TPU v7x, 512 devices: a whole 4x4x16 slice. The times are simulated.
512 devices in a mesh: section: 2 (over x_lo), expert: 64 (over z, x_hi, core), dp: 4 (over y).
Axes of the slice: x: 4 (x_hi: 2, x_lo: 2; x = x_hi * 2 + x_lo), y: 4, z: 16, core: 2. Of those that a mesh axis runs over, the one named last changes fastest.
Arguments:
- tokens: bfloat16 [2, 32768, 3584], P('section', ('expert', 'dp')), may hold values from -6 to 6
- grad_out: bfloat16 [2, 32768, 3584], P('section', ('expert', 'dp')), may hold values from -6 to 6
- expert_ids: int32 [2, 32768, 2], P('section', ('expert', 'dp')), may hold values from 0 to 31, all different within a row; in each aligned block of 128 rows (0 to 127, 128 to 255, ..., all dimensions but the last counted through in order) at most 9 rows name the same one
- gate_values: float32 [2, 32768, 2], P('section', ('expert', 'dp')), may hold values from 0.1 to 1
- w_in: bfloat16 [2, 64, 1792, 1024], P('section', 'expert', None, 'dp'), may hold values from -0.09375 to 0.09375
- w_out_t: bfloat16 [2, 64, 1792, 1024], P('section', 'expert', None, 'dp'), may hold values from -0.1875 to 0.1875
Outputs:
- handed_grad: bfloat16 [2, 32768, 3584], P('section', ('expert', 'dp'))
Inputs may be any that keep to these rules, and one draw needn't show every extreme that they name: `expert_ids`: each token names 2 different experts; in each aligned block of 128 tokens (the tokens of one device) no expert is named more than 9 times, a bound that some block reaches.
All inputs are finite; a program needn't handle non-finite values.
Results may differ from a plain program's by a relative error of at most 0.0051.
Values may be sent and summed in bfloat16 or wider, within the bound.
A program may use at most 128 MiB of HBM per device.

v0:
```python
import jax
import jax.numpy as jnp
from jax import lax
from jax.sharding import PartitionSpec as P


def partner(value, axis, apart):
    mask = 2**apart
    pairs = [(source, source ^ mask) for source in range(lax.axis_size(axis))]
    return lax.ppermute(value, axis, pairs)


def slot_layout(ids, experts):
    flat_ids = ids.reshape(-1)
    onehot = (flat_ids[:, None] == jnp.arange(experts, dtype=jnp.int32)[None, :]).astype(jnp.int32)
    before = jnp.cumsum(onehot, axis=0) - onehot
    rank = jnp.sum(before * onehot, axis=1)
    return (flat_ids, rank)


def silu_slope(pre):
    sig = jax.nn.sigmoid(pre)
    return sig * (1.0 + pre * (1.0 - sig))


def body(tokens, grad_out, expert_ids, gate_values, w_in, w_out_t):
    tok_rows = tokens[0]
    grad_rows = grad_out[0]
    ids = expert_ids[0]
    gates = gate_values[0]
    tok_dev, width = tok_rows.shape
    top = ids.shape[1]
    half = width // 2
    n_expert = lax.axis_size("expert")
    experts = n_expert // 2
    capacity = min(tok_dev, max(2, tok_dev * top // experts + 1))
    w_in_full, w_out_full = (
        lax.all_gather(w_in[0, 0], "dp", axis=1, tiled=True),
        lax.all_gather(w_out_t[0, 0], "dp", axis=1, tiled=True),
    )
    flat_ids, rank = slot_layout(ids, experts)
    source = jnp.arange(tok_dev * top, dtype=jnp.int32) // top
    scaled = (gates.reshape(-1)[:, None] * grad_rows[source].astype(jnp.float32)).astype(
        jnp.bfloat16
    )
    empty = jnp.zeros((experts, 2, capacity, half), jnp.bfloat16)
    tok_send = empty.at[flat_ids, :, rank].set(tok_rows[source].reshape(-1, 2, half))
    grad_send = empty.at[flat_ids, :, rank].set(scaled.reshape(-1, 2, half))
    tok_send = tok_send.reshape(n_expert, capacity, half)
    grad_send = grad_send.reshape(n_expert, capacity, half)
    tok_in = lax.all_to_all(tok_send, "expert", split_axis=0, concat_axis=0, tiled=True)
    grad_in = lax.all_to_all(grad_send, "expert", split_axis=0, concat_axis=0, tiled=True)
    sources, slots, _ = tok_in.shape
    tok_flat = tok_in.reshape(sources * slots, half)
    grad_flat = grad_in.reshape(sources * slots, half)
    pre_part = jnp.dot(tok_flat, w_in_full, preferred_element_type=jnp.float32).astype(jnp.bfloat16)
    hid_part = jnp.dot(grad_flat, w_out_full, preferred_element_type=jnp.float32).astype(
        jnp.bfloat16
    )
    pre_other, hid_other = partner((pre_part, hid_part), "expert", 0)
    pre = pre_part.astype(jnp.float32) + pre_other.astype(jnp.float32)
    hidden = hid_part.astype(jnp.float32) + hid_other.astype(jnp.float32)
    act_grad = (hidden * silu_slope(pre)).astype(jnp.bfloat16)
    back = lax.dot_general(
        act_grad, w_in_full, (((1,), (1,)), ((), ())), preferred_element_type=jnp.float32
    )
    back = back.astype(jnp.bfloat16).reshape(sources, slots, half)
    returned = lax.all_to_all(back, "expert", split_axis=0, concat_axis=0, tiled=True)
    returned = returned.reshape(experts, 2, capacity, half)
    rows_back = returned[flat_ids, :, rank].reshape(tok_dev, top, width).astype(jnp.float32)
    expert_sum = jnp.sum(rows_back, axis=1)
    own_grad = (grad_rows.astype(jnp.float32) + expert_sum).astype(jnp.bfloat16)
    handed = partner(own_grad, "section", 0)
    return handed[None]


def solution(mesh):
    return jax.shard_map(
        body,
        mesh=mesh,
        in_specs=(
            P("section", ("expert", "dp"), None),
            P("section", ("expert", "dp"), None),
            P("section", ("expert", "dp"), None),
            P("section", ("expert", "dp"), None),
            P("section", "expert", None, "dp"),
            P("section", "expert", None, "dp"),
        ),
        out_specs=P("section", ("expert", "dp"), None),
        check_vma=False,
    )
```

profile of v0, /device:TPU:1, one launch (start us, length us, event | category | flops | bytes accessed | tf_op | source)
XLA Modules:
  0.0 653.6 jit_solution(3123240296850334480)
XLA Ops:
  6.5 0.0 copy-start
  6.5 0.9 copy.27
  7.4 0.1 eq.29
  7.5 0.1 eq.25
  7.7 0.1 reshape_squeeze.3
  7.9 0.6 reduce-window.6
  8.4 0.2 slice_reduce_fusion
  8.7 0.0 copy-done
  8.7 1.7 gather_fusion.1
  10.4 1.5 reshape.175
  11.9 0.1 fusion.18
  12.0 1.1 broadcast_in_dim.4.clone
  13.1 24.0 %scatter_fusion.1 = bf16[32,2,9,1792]{3,1,2,0:T(2,128)(2,1)S(1)} fusion(bf16[32,2,9,1792]{3,1,2,0:T(2,128)(2,1)S(1)} %broadcast_in_dim.4.clone, s32[256]{0:T(256)S(1)} %bitcast.48, bf16[256,2,1792]{2,1,0:T(2,128)(2,1)} %reshape.175), kind=kCustom, calls=%fused_computation.4 | custom fusion | bytes 5507072 | tf_op jit(solution)/shard_map/scatter | solution.py:47
  37.1 2.5 copy.39
  39.6 19.8 %all-to-all-start.1 = ((bf16[64,9,1792]{2,1,0:T(8,128)(2,1)}), bf16[64,9,1792]{2,1,0:T(8,128)(2,1)}, u32[]{:S(2)}, u32[]{:S(2)}) async-start(bf16[64,9,1792]{2,1,0:T(8,128)(2,1)} %bitcast.51), calls=%async_computation.1 | async-start | bytes 7340032 | tf_op jit(solution)/shard_map/all_to_all | solution.py:51
  59.4 0.0 copy-start.2
  59.4 0.0 all-gather.7.cloned.1.call-start
  59.4 0.7 all-gather.7.cloned.1.call-update
  60.1 0.4 copy-done.2
  60.5 3.0 gather_fusion
  63.5 0.0 copy-start.3
  63.5 5.3 reshape.143
  68.9 0.0 copy-done.3
  68.9 0.1 copy.31
  69.0 0.1 mul.24
  69.1 4.6 multiply_convert_fusion
  73.8 2.4 broadcast_in_dim.4.clone.1
  76.1 35.3 %scatter_fusion = bf16[32,2,9,1792]{3,1,2,0:T(2,128)(2,1)} fusion(bf16[32,2,9,1792]{3,1,2,0:T(2,128)(2,1)} %broadcast_in_dim.4.clone.1, s32[256]{0:T(256)S(1)} %bitcast.49, bf16[256,2,1792]{2,1,0:T(2,128)(2,1)} %multiply_convert_fusion), kind=kCustom, calls=%fused_computation.3 | custom fusion | bytes 5507072 | tf_op jit(solution)/shard_map/scatter | solution.py:48
  111.5 4.1 copy.38
  115.6 107.3 %all-to-all-done.1 = bf16[64,9,1792]{2,1,0:T(8,128)(2,1)} async-done(((bf16[64,9,1792]{2,1,0:T(8,128)(2,1)}), bf16[64,9,1792]{2,1,0:T(8,128)(2,1)}, u32[]{:S(2)}, u32[]{:S(2)}) %all-to-all-start.1) | async-done | bytes 2064416 | tf_op jit(solution)/shard_map/all_to_all | solution.py:51
  222.9 10.5 %all-to-all-start = ((bf16[64,9,1792]{2,1,0:T(8,128)(2,1)}), bf16[64,9,1792]{2,1,0:T(8,128)(2,1)}, u32[]{:S(2)}, u32[]{:S(2)}) async-start(bf16[64,9,1792]{2,1,0:T(8,128)(2,1)} %bitcast.52), calls=%async_computation | async-start | bytes 7340032 | tf_op jit(solution)/shard_map/all_to_all | solution.py:52
  233.4 0.0 all-gather.5.cloned.1.call-start
  233.5 0.7 all-gather.5.cloned.1.call-update
  234.2 4.5 reshape.140
  238.7 0.0 all-gather.7.cloned.1.call-done
  238.7 5.0 fusion.12
  243.6 2.5 collective-permute-start.1
  246.2 151.1 %all-to-all-done = bf16[64,9,1792]{2,1,0:T(8,128)(2,1)} async-done(((bf16[64,9,1792]{2,1,0:T(8,128)(2,1)}), bf16[64,9,1792]{2,1,0:T(8,128)(2,1)}, u32[]{:S(2)}, u32[]{:S(2)}) %all-to-all-start) | async-done | bytes 2064416 | tf_op jit(solution)/shard_map/all_to_all | solution.py:52
  397.3 4.5 reshape.137
  401.8 0.0 all-gather.5.cloned.1.call-done
  401.8 0.0 copy-start.4
  401.8 5.1 fusion.9
  406.9 7.1 %collective-permute-start = (bf16[576,1024]{1,0:T(8,128)(2,1)S(1)}, bf16[576,1024]{1,0:T(8,128)(2,1)S(1)}, u32[]{:S(2)}, u32[]{:S(2)}) collective-permute-start(bf16[576,1024]{1,0:T(8,128)(2,1)S(1)} %fusion.9), channel_id=1, source_target_pairs={{0,4},{4,0},{8,12},{12,8},{16,20},{20,16},{24,28},{28,24},{32,36},... | collective-permute-start | bytes 3538952 | tf_op jit(solution)/shard_map/ppermute | solution.py:10
  414.0 0.0 collective-permute-done.1
  414.0 2.4 collective-permute-done
  416.4 0.0 copy-done.4
  416.4 5.9 fusion.6
  422.3 4.4 reshape.141
  426.7 171.8 %all_to_all.15 = bf16[64,9,1792]{2,1,0:T(8,128)(2,1)S(1)} all-to-all(bf16[64,9,1792]{2,1,0:T(8,128)(2,1)} %reshape.141), channel_id=1, replica_groups=mesh['section'=2,'expert'=64,'dp'=4] {'expert'}, dimensions={0} | all-to-all | bytes 4128768 | tf_op jit(solution)/shard_map/all_to_all | solution.py:68
  598.5 3.0 copy.37
  601.5 7.3 %gather_fusion.2 = bf16[256,2,1792]{2,1,0:T(2,128)(2,1)} fusion(bf16[32,2,9,1792]{3,1,2,0:T(2,128)(2,1)} %copy.37, s32[256]{0:T(256)S(1)} %bitcast.50), kind=kCustom, calls=%fused_computation.2 | custom fusion | bytes 3672064 | tf_op jit(solution)/shard_map/gather | solution.py:70
  608.8 6.3 reshape.144
  615.1 0.0 copy-start.1
  615.1 7.7 %reduce_sum.22 = f32[128,3584]{1,0:T(8,128)} reduce(f32[128,2,3584]{2,1,0:T(2,128)} %reshape.144, f32[]{:T(128)} %constant.33.clone.1), dimensions={1}, to_apply=%region_5.6 | reduce | flops 458752 | bytes 5505028 | tf_op jit(solution)/shard_map/reduce_sum | solution.py:71
  622.8 1.7 add_convert_fusion
  624.5 2.2 collective-permute-start.2
  626.7 19.1 %collective-permute-done.2 = bf16[128,3584]{1,0:T(8,128)(2,1)S(1)} collective-permute-done((bf16[128,3584]{1,0:T(8,128)(2,1)S(1)}, bf16[128,3584]{1,0:T(8,128)(2,1)S(1)}, u32[]{:S(2)}, u32[]{:S(2)}) %collective-permute-start.2) | collective-permute-done | bytes 917536 | tf_op jit(solution)/shard_map/ppermute | solution.py:10
  645.9 0.9 copy.49
  646.8 0.0 copy-done.1
  (6 shorter events, 0.1 us)
Async XLA Ops:
  6.5 2.2 copy-start
  39.6 183.3 %all-to-all-start.1 = ((bf16[64,9,1792]{2,1,0:T(8,128)(2,1)}), bf16[64,9,1792]{2,1,0:T(8,128)(2,1)}, u32[]{:S(2)}, u32[]{:S(2)}) async-start(bf16[64,9,1792]{2,1,0:T(8,128)(2,1)} %bitcast.51), calls=%async_computation.1 | async-start | bytes 7340032 | tf_op jit(solution)/shard_map/all_to_all | solution.py:51
  59.4 1.2 copy-start.2
  59.4 179.3 %all-gather.7.cloned.1.call-start = ((), (), s32[]{:S(2)}) async-start(), calls=%async_computation.4 | async-start | bytes 4587520 | tf_op jit(solution)/shard_map/all_gather | solution.py:38
  63.5 5.4 copy-start.3
  222.9 174.4 %all-to-all-start = ((bf16[64,9,1792]{2,1,0:T(8,128)(2,1)}), bf16[64,9,1792]{2,1,0:T(8,128)(2,1)}, u32[]{:S(2)}, u32[]{:S(2)}) async-start(bf16[64,9,1792]{2,1,0:T(8,128)(2,1)} %bitcast.52), calls=%async_computation | async-start | bytes 7340032 | tf_op jit(solution)/shard_map/all_to_all | solution.py:52
  233.4 168.3 %all-gather.5.cloned.1.call-start = ((), (), s32[]{:S(2)}) async-start(), calls=%async_computation.3 | async-start | bytes 4587520 | tf_op jit(solution)/shard_map/all_gather | solution.py:39
  243.6 170.4 %collective-permute-start.1 = (bf16[576,1024]{1,0:T(8,128)(2,1)S(1)}, bf16[576,1024]{1,0:T(8,128)(2,1)}, u32[]{:S(2)}, u32[]{:S(2)}) collective-permute-start(bf16[576,1024]{1,0:T(8,128)(2,1)S(1)} %fusion.12), channel_id=1, source_target_pairs={{0,4},{4,0},{8,12},{12,8},{16,20},{20,16},{24,28},{28,24},{32,36},... | collective-permute-start | bytes 3538952 | tf_op jit(solution)/shard_map/ppermute | solution.py:10
  401.8 14.7 %copy-start.4 = (bf16[1,1,1792,1024]{3,2,1,0:T(8,128)(2,1)S(1)}, bf16[1,1,1792,1024]{3,2,1,0:T(8,128)(2,1)}, u32[]{:S(2)}) copy-start(bf16[1,1,1792,1024]{3,2,1,0:T(8,128)(2,1)} %all-gather.7.cloned.1.call-done) | copy-start | bytes 11010052
  406.9 9.6 %collective-permute-start = (bf16[576,1024]{1,0:T(8,128)(2,1)S(1)}, bf16[576,1024]{1,0:T(8,128)(2,1)S(1)}, u32[]{:S(2)}, u32[]{:S(2)}) collective-permute-start(bf16[576,1024]{1,0:T(8,128)(2,1)S(1)} %fusion.9), channel_id=1, source_target_pairs={{0,4},{4,0},{8,12},{12,8},{16,20},{20,16},{24,28},{28,24},{32,36},... | collective-permute-start | bytes 3538952 | tf_op jit(solution)/shard_map/ppermute | solution.py:10
  615.1 31.7 %copy-start.1 = (bf16[1,128,3584]{2,1,0:T(8,128)(2,1)S(1)}, bf16[1,128,3584]{2,1,0:T(8,128)(2,1)}, u32[]{:S(2)}) copy-start(bf16[1,128,3584]{2,1,0:T(8,128)(2,1)} %param.6) | copy-start | bytes 2752516
  624.5 21.4 %collective-permute-start.2 = (bf16[128,3584]{1,0:T(8,128)(2,1)S(1)}, bf16[128,3584]{1,0:T(8,128)(2,1)S(1)}, u32[]{:S(2)}, u32[]{:S(2)}) collective-permute-start(bf16[128,3584]{1,0:T(8,128)(2,1)S(1)} %add_convert_fusion), channel_id=1, source_target_pairs={{0,256},{256,0},{1,257},{257,1},{2,258},{258,2},{3,259},{259,3},{4... | collective-permute-start | bytes 2752520 | tf_op jit(solution)/shard_map/ppermute | solution.py:10
Sparse Core Ops, SparseCore 0:
  62.3 55.1 all-gather.6
  236.4 55.2 all-gather.4
where the time goes:
time: 658 us; the launch traced here: 654 us
  waiting for transfers between devices  281 us (43%)
  blocking collectives  172 us (26%)
  local copies, waits for them, and re-layouts  114 us (17%)
  starting transfers between devices  42.3 us (6%)
  matrix products  15.9 us (2%)
  other arithmetic  14.7 us (2%)
  between operations  13.6 us (2%)
    all_to_all x1, blocking collectives, body(): lax.all_to_all(back, 'expert', split_axis=0, concat_axis=0, tiled=True)  172 us
    all_to_all x1, waiting for transfers between devices, body(): lax.all_to_all(grad_send, 'expert', split_axis=0, concat_axis=0, tiled=True)  151 us
    all_to_all x1, waiting for transfers between devices, body(): lax.all_to_all(tok_send, 'expert', split_axis=0, concat_axis=0, tiled=True)  107 us
    scatter x1, local copies, waits for them, and re-layouts, body(): grad_send = empty.at[flat_ids, :, rank].set(scaled.reshape(-1, 2, half))  35.3 us
    scatter x1, local copies, waits for them, and re-layouts, body(): empty.at[flat_ids, :, rank].set(tok_rows[source].reshape(-1, 2, half))  24 us
    ppermute x3, waiting for transfers between devices, partner(): return lax.ppermute(value, axis, pairs)  21.6 us
    all_to_all x1, starting transfers between devices, body(): lax.all_to_all(tok_send, 'expert', split_axis=0, concat_axis=0, tiled=True)  19.8 us
  transfers between devices with their start and end apart: 7, of which 4 were waited for; matrix products, arithmetic and copies ran while one was open for 11% of the time, Pallas kernels for 0%

commit v1 on v0

v1 whole, which is shorter than its diff:
```python
import functools

import jax
import jax.numpy as jnp
from jax import lax
from jax.experimental import pallas as pl
from jax.experimental.pallas import tpu as pltpu
from jax.sharding import PartitionSpec as P

MESH = pl.DeviceIdType.MESH
F32 = jnp.float32
BF16 = jnp.bfloat16
GROUP = 8


def silu_slope(pre):
    sig = 1.0 / (1.0 + jnp.exp(-pre))
    return sig * (1.0 + pre * (1.0 - sig))


def kernel(
    ring,
    n_dp,
    tok_ref,
    grad_ref,
    ids_ref,
    gate_ref,
    win_ref,
    wout_ref,
    out_ref,
    xg,
    partner_grad,
    combine,
    partner_combine,
    send_a,
    send_b,
    recv_a,
    recv_b,
    back_a,
    back_b,
    home_a,
    home_b,
    w_full,
    v_full,
    act,
    row_scr,
    home_scr,
    load_sem,
    send_a_sem,
    send_b_sem,
    recv_a_sem,
    recv_b_sem,
    back_a_sem,
    back_b_sem,
    home_a_sem,
    home_b_sem,
    hand_send_sem,
    hand_recv_sem,
    wdp_send_sem,
    wdp_recv_sem,
    wcore_send_sem,
    wcore_recv_sem,
):
    n_tok, width = tok_ref.shape
    half = width // 2
    quarter = win_ref.shape[1]
    chips = 2 * ring
    chunks = chips // GROUP
    section = lax.axis_index("section")
    me = lax.axis_index("expert")
    dp = lax.axis_index("dp")
    core = lax.rem(me, 2)
    my_chip = me // 2
    my_xh = lax.rem(my_chip, 2)
    my_z = my_chip // 2
    other_section = 1 - section
    other_core = me + 1 - 2 * core

    barrier = pltpu.get_barrier_semaphore()

    @pl.loop(0, chips)
    def _(chip):
        @pl.when(chip != my_chip)
        def _():
            pl.semaphore_signal(
                barrier, inc=1, device_id={"expert": 2 * chip + core}, device_id_type=MESH
            )

        pl.semaphore_signal(
            barrier,
            inc=1,
            device_id={"section": other_section, "expert": 2 * chip + core},
            device_id_type=MESH,
        )

    for step in range(1, n_dp):
        pl.semaphore_signal(
            barrier, inc=1, device_id={"dp": lax.rem(dp + step, n_dp)}, device_id_type=MESH
        )
    pl.semaphore_signal(barrier, inc=1, device_id={"expert": other_core}, device_id_type=MESH)

    load_tok = pltpu.make_async_copy(tok_ref, xg.at[pl.ds(0, n_tok)], load_sem.at[0])
    load_grad = pltpu.make_async_copy(grad_ref, xg.at[pl.ds(n_tok, n_tok)], load_sem.at[1])
    load_win = pltpu.make_async_copy(win_ref, w_full.at[dp, core], load_sem.at[2])
    load_wout = pltpu.make_async_copy(wout_ref, v_full.at[dp, core], load_sem.at[3])
    load_tok.start()
    load_grad.start()
    load_win.start()
    load_wout.start()

    ids = jnp.concatenate([ids_ref[0:1, :], ids_ref[1:2, :]], axis=1)
    flat = 2 * n_tok
    hot = (lax.broadcasted_iota(jnp.int32, (chips, flat), 0) == ids).astype(F32)
    earlier = (
        lax.broadcasted_iota(jnp.int32, (flat, flat), 0)
        < lax.broadcasted_iota(jnp.int32, (flat, flat), 1)
    ).astype(F32)
    before = jnp.dot(hot.astype(BF16), earlier.astype(BF16), preferred_element_type=F32)
    rank = jnp.sum(hot * before, axis=0, keepdims=True).astype(jnp.int32)
    apart = (ids // 2 - my_z + ring) % ring
    hops = jnp.minimum(apart, ring - apart)
    place = 2 * (ring // 2 - hops) - (apart < ring // 2).astype(jnp.int32)
    unit = 2 * place + ids % 2
    extra = rank >= GROUP
    full_rows = chips * 2 * GROUP
    row_x = jnp.where(extra, full_rows + 2 * unit, unit * 2 * GROUP + rank)
    row_g = jnp.where(extra, row_x + 1, row_x + GROUP)
    slot = jnp.where(extra, chips * GROUP + ids, ids * GROUP + rank)

    slot_rows = combine.shape[1]
    slot_iota = lax.broadcasted_iota(jnp.int32, (slot_rows, n_tok), 0)
    picks = (slot_iota == slot[:, :n_tok]).astype(F32) + (slot_iota == slot[:, n_tok:]).astype(F32)
    combine[...] = jnp.transpose(picks).astype(BF16)

    pl.semaphore_wait(barrier, 2 * chips - 1 + n_dp)

    def weight_send(mat, y_from, target, to_core):
        full = (w_full, v_full)[mat]
        if to_core:
            return pltpu.make_async_remote_copy(
                src_ref=full.at[y_from, core],
                dst_ref=full.at[y_from, core],
                send_sem=wcore_send_sem.at[mat, y_from],
                recv_sem=wcore_recv_sem.at[mat, y_from],
                device_id={"expert": other_core},
                device_id_type=MESH,
            )
        return pltpu.make_async_remote_copy(
            src_ref=(win_ref, wout_ref)[mat],
            dst_ref=full.at[dp, core],
            send_sem=wdp_send_sem.at[mat, target],
            recv_sem=wdp_recv_sem.at[mat, dp],
            device_id={"dp": target},
            device_id_type=MESH,
        )

    steps = [s for pair in zip(range(1, n_dp), range(n_dp - 1, 0, -1)) for s in pair]
    steps = list(dict.fromkeys(steps))
    for step in steps:
        for mat in range(2):
            weight_send(mat, None, lax.rem(dp + step, n_dp), False).start()

    def hand(which):
        return pltpu.make_async_remote_copy(
            src_ref=(grad_ref, combine)[which],
            dst_ref=(partner_grad, partner_combine)[which],
            send_sem=hand_send_sem.at[which],
            recv_sem=hand_recv_sem.at[which],
            device_id={"section": other_section},
            device_id_type=MESH,
        )

    hand(0).start()
    hand(1).start()

    load_tok.wait()
    load_grad.wait()

    def shift_of(place):
        odd = place % 2
        hop = ring // 2 - (place + odd) // 2
        return jnp.where(odd == 1, hop, ring - hop) % ring

    def mirror_of(place):
        odd = place % 2
        inner = jnp.where(odd == 1, place + 1, place - 1)
        return jnp.where((place == 0) | (place == ring - 1), place, inner)

    def dispatch(unit, own):
        place = unit // 2
        xh = unit % 2
        chip = 2 * ((my_z + shift_of(place)) % ring) + xh
        there = 2 * mirror_of(place) + my_xh
        pair_a = (send_a.at[unit], recv_a.at[there // GROUP, there % GROUP])
        pair_b = (send_b.at[unit], recv_b.at[there])
        pairs = (
            (pair_a, (send_a_sem, recv_a_sem)),
            (pair_b, (send_b_sem, recv_b_sem)),
        )
        if own:
            return [
                pltpu.make_async_copy(*pair, sems[1].at[there]) for pair, sems in pairs
            ]
        return [
            pltpu.make_async_remote_copy(
                src_ref=pair[0],
                dst_ref=pair[1],
                send_sem=sems[0].at[unit],
                recv_sem=sems[1].at[there],
                device_id={"expert": 2 * chip + core},
                device_id_type=MESH,
            )
            for pair, sems in pairs
        ]

    own_unit = 2 * (ring - 1) + my_xh
    rows = GROUP * 2 * GROUP
    block = 512 if width % 512 == 0 else 256

    @pl.loop(0, chunks)
    def _(chunk):
        local_row = lax.broadcasted_iota(jnp.int32, (rows + 2 * GROUP, 1), 0)
        spare = local_row >= rows
        row_id = jnp.where(
            spare, full_rows + chunk * 2 * GROUP + local_row - rows, chunk * rows + local_row
        )
        is_x = jnp.where(spare, local_row % 2, local_row % (2 * GROUP) // GROUP) == 0
        x0 = row_id == row_x[:, :n_tok]
        x1 = row_id == row_x[:, n_tok:]
        g0 = row_id == row_g[:, :n_tok]
        g1 = row_id == row_g[:, n_tok:]
        pick = jnp.concatenate(
            [x0.astype(F32) + x1.astype(F32), g0.astype(F32) + g1.astype(F32)], axis=1
        ).astype(BF16)
        gate = jnp.where(g0, gate_ref[0:1, :], 0.0) + jnp.where(g1, gate_ref[1:2, :], 0.0)
        gate = jnp.sum(gate, axis=1, keepdims=True)
        scale = jnp.where(is_x, 1.0, gate)
        for lane in range(0, width, block):
            part = jnp.dot(pick, xg[:, lane : lane + block], preferred_element_type=F32) * scale
            send_a[pl.ds(chunk * GROUP, GROUP), :, lane : lane + block] = (
                part[:rows].astype(BF16).reshape(GROUP, 2 * GROUP, block)
            )
            row_scr[:, lane : lane + block] = part[rows:]
        for i in range(GROUP):
            send_b[chunk * GROUP + i] = row_scr[2 * i : 2 * i + 2, :].astype(BF16)

        @pl.loop(0, GROUP)
        def _(i):
            unit = chunk * GROUP + i
            own = unit == own_unit

            @pl.when(own)
            def _():
                for copy in dispatch(unit, True):
                    copy.start()

            @pl.when(jnp.logical_not(own))
            def _():
                for copy in dispatch(unit, False):
                    copy.start()

    load_win.wait()
    load_wout.wait()
    for mat in range(2):
        weight_send(mat, dp, None, True).start()
    for step in steps:
        y_from = lax.rem(dp + n_dp - step, n_dp)
        for mat in range(2):
            pltpu.make_async_remote_copy(
                src_ref=(win_ref, wout_ref)[mat],
                dst_ref=(w_full, v_full)[mat].at[y_from, core],
                send_sem=wdp_send_sem.at[mat, y_from],
                recv_sem=wdp_recv_sem.at[mat, y_from],
                device_id={"dp": y_from},
                device_id_type=MESH,
            ).wait_recv()
            weight_send(mat, y_from, None, True).start()
    for y_from in range(n_dp):
        for mat in range(2):
            full = (w_full, v_full)[mat]
            pltpu.make_async_remote_copy(
                src_ref=full.at[y_from, 1 - core],
                dst_ref=full.at[y_from, 1 - core],
                send_sem=wcore_send_sem.at[mat, y_from],
                recv_sem=wcore_recv_sem.at[mat, y_from],
                device_id={"expert": other_core},
                device_id_type=MESH,
            ).wait_recv()

    def give_back(unit):
        chip = 2 * ((my_z + shift_of(unit // 2)) % ring) + unit % 2
        return [
            pltpu.make_async_remote_copy(
                src_ref=source.at[unit],
                dst_ref=home.at[my_chip],
                send_sem=sems[0].at[unit],
                recv_sem=sems[1].at[my_chip],
                device_id={"section": other_section, "expert": 2 * chip + core},
                device_id_type=MESH,
            )
            for source, home, sems in (
                (back_a, home_a, (back_a_sem, home_a_sem)),
                (back_b, home_b, (back_b_sem, home_b_sem)),
            )
        ]

    tall = 2 * GROUP * (GROUP + 1)
    short = GROUP * (GROUP + 1)

    @pl.loop(0, chunks)
    def _(chunk):
        @pl.loop(0, GROUP)
        def _(i):
            unit = chunk * GROUP + i
            a_ref = recv_a.at[chunk, i]
            pltpu.make_async_copy(a_ref, a_ref, recv_a_sem.at[unit]).wait()
            b_ref = recv_b.at[unit]
            pltpu.make_async_copy(b_ref, b_ref, recv_b_sem.at[unit]).wait()

        for i in range(GROUP):
            pair = recv_b[chunk * GROUP + i].astype(F32)
            row_scr[i : i + 1, :] = pair[0:1]
            row_scr[GROUP + i : GROUP + i + 1, :] = pair[1:2]
        recv_a[chunk, GROUP] = row_scr[...].astype(BF16)

        @pl.loop(0, n_dp)
        def _(y):
            def product(full, first):
                total = None
                for h in range(2):
                    left = recv_a[chunk, :, :, h * half : (h + 1) * half].reshape(tall, half)
                    part = jnp.dot(left, full[y, h], preferred_element_type=F32)
                    part = part.reshape(GROUP + 1, 2 * GROUP, quarter)
                    part = part[:, first : first + GROUP, :].astype(BF16).astype(F32)
                    total = part if total is None else total + part
                return total

            pre = product(w_full, 0)
            hid = product(v_full, GROUP)
            act[y] = (hid * silu_slope(pre)).reshape(short, quarter).astype(BF16)

        lanes = 256 if half % 256 == 0 else half
        for h in range(2):
            for lane in range(0, half, lanes):
                total = None
                for y in range(n_dp):
                    part = lax.dot_general(
                        act[y],
                        w_full[y, h, lane : lane + lanes, :],
                        (((1,), (1,)), ((), ())),
                        preferred_element_type=F32,
                    )
                    total = part if total is None else total + part
                left = h * half + lane
                back_a[pl.ds(chunk * GROUP, GROUP), :, left : left + lanes] = (
                    total[: GROUP * GROUP].reshape(GROUP, GROUP, lanes).astype(BF16)
                )
                row_scr[:GROUP, left : left + lanes] = total[GROUP * GROUP :]
        for i in range(GROUP):
            back_b[chunk * GROUP + i] = jnp.concatenate(
                [row_scr[i : i + 1, :half], row_scr[i : i + 1, half:]], axis=0
            ).astype(BF16)

        @pl.loop(0, GROUP)
        def _(i):
            for copy in give_back(chunk * GROUP + i):
                copy.start()

    hand(0).wait_recv()
    hand(1).wait_recv()

    @pl.loop(0, chips)
    def _(chip):
        a_ref = home_a.at[chip]
        pltpu.make_async_copy(a_ref, a_ref, home_a_sem.at[chip]).wait()
        b_ref = home_b.at[chip]
        pltpu.make_async_copy(b_ref, b_ref, home_b_sem.at[chip]).wait()

    for chip in range(chips):
        pair = home_b[chip].astype(F32)
        home_scr[chip : chip + 1, :half] = pair[0:1]
        home_scr[chip : chip + 1, half:] = pair[1:2]
    for lane in range(0, width, block):
        span = slice(lane, lane + block)
        main = home_a[:, :, span].astype(F32).reshape(chips * GROUP, block).astype(BF16)
        total = jnp.dot(
            partner_combine[:, : chips * GROUP], main, preferred_element_type=F32
        ) + jnp.dot(
            partner_combine[:, chips * GROUP : chips * GROUP + chips],
            home_scr[:, span].astype(BF16),
            preferred_element_type=F32,
        )
        out_ref[:, span] = (partner_grad[:, span].astype(F32) + total).astype(BF16)

    hand(0).wait_send()
    hand(1).wait_send()
    for step in range(1, n_dp):
        for mat in range(2):
            weight_send(mat, None, lax.rem(dp + step, n_dp), False).wait_send()
    for y_from in range(n_dp):
        for mat in range(2):
            weight_send(mat, y_from, None, True).wait_send()

    @pl.loop(0, chips)
    def _(unit):
        @pl.when(unit != own_unit)
        def _():
            for copy in dispatch(unit, False):
                copy.wait_send()

        for copy in give_back(unit):
            copy.wait_send()


def call(ring, n_dp, tokens, grads, ids, gates, w_in, w_out):
    n_tok, width = tokens.shape
    half = width // 2
    quarter = w_in.shape[1]
    chips = 2 * ring
    chunks = chips // GROUP
    slot_rows = -(-(chips * (GROUP + 1)) // 128) * 128
    dma = pltpu.SemaphoreType.DMA
    any_spec = pl.BlockSpec(memory_space=pl.ANY)
    vmem_spec = pl.BlockSpec(memory_space=pltpu.VMEM)
    return pl.pallas_call(
        functools.partial(kernel, ring, n_dp),
        out_shape=jax.ShapeDtypeStruct((n_tok, width), BF16),
        in_specs=[any_spec, any_spec, vmem_spec, vmem_spec, any_spec, any_spec],
        out_specs=vmem_spec,
        scratch_shapes=[
            pltpu.VMEM((2 * n_tok, width), BF16),
            pltpu.VMEM((n_tok, width), BF16),
            pltpu.VMEM((n_tok, slot_rows), BF16),
            pltpu.VMEM((n_tok, slot_rows), BF16),
            pltpu.VMEM((chips, 2 * GROUP, width), BF16),
            pltpu.VMEM((chips, 2, width), BF16),
            pltpu.VMEM((chunks, GROUP + 1, 2 * GROUP, width), BF16),
            pltpu.VMEM((chips, 2, width), BF16),
            pltpu.VMEM((chips, GROUP, width), BF16),
            pltpu.VMEM((chips, 2, half), BF16),
            pltpu.VMEM((chips, GROUP, width), BF16),
            pltpu.VMEM((chips, 2, half), BF16),
            pltpu.VMEM((n_dp, 2, half, quarter), BF16),
            pltpu.VMEM((n_dp, 2, half, quarter), BF16),
            pltpu.VMEM((n_dp, GROUP * (GROUP + 1), quarter), BF16),
            pltpu.VMEM((2 * GROUP, width), F32),
            pltpu.VMEM((chips, width), F32),
            dma((4,)),
            dma((chips,)),
            dma((chips,)),
            dma((chips,)),
            dma((chips,)),
            dma((chips,)),
            dma((chips,)),
            dma((chips,)),
            dma((chips,)),
            dma((2,)),
            dma((2,)),
            dma((2, n_dp)),
            dma((2, n_dp)),
            dma((2, n_dp)),
            dma((2, n_dp)),
        ],
        compiler_params=pltpu.CompilerParams(
            collective_id=0, has_side_effects=True, vmem_limit_bytes=56 * 1024 * 1024
        ),
        name="routed_backward",
    )(tokens, grads, ids, gates, w_in, w_out)


def solution(mesh):
    ring = mesh.shape["expert"] // 4
    n_dp = mesh.shape["dp"]

    def body(tokens, grad_out, expert_ids, gate_values, w_in, w_out_t):
        handed = call(
            ring,
            n_dp,
            tokens[0],
            grad_out[0],
            expert_ids[0].T,
            gate_values[0].T,
            w_in[0, 0],
            w_out_t[0, 0],
        )
        return handed[None]

    return jax.shard_map(
        body,
        mesh=mesh,
        in_specs=(
            P("section", ("expert", "dp"), None),
            P("section", ("expert", "dp"), None),
            P("section", ("expert", "dp"), None),
            P("section", ("expert", "dp"), None),
            P("section", "expert", None, "dp"),
            P("section", "expert", None, "dp"),
        ),
        out_specs=P("section", ("expert", "dp"), None),
        check_vma=False,
    )
```

time: 658 us -> 293 us (0.45)
  Pallas kernels: 0 us -> 290 us
  waiting for transfers between devices: 281 us -> 0 us
  blocking collectives: 172 us -> 0 us
  local copies, waits for them, and re-layouts: 114 us -> 2.16 us
  starting transfers between devices: 42.3 us -> 0 us
  matrix products: 15.9 us -> 0 us
  other arithmetic: 14.7 us -> 0 us
  between operations: 13.6 us -> 0.01 us
    pallas_call x0 -> x1, Pallas kernels: none -> 290 us  [call(): pl.pallas_call(functools.partial(kernel, ring, n_dp), out_shape=jax.Shape...]
    all_to_all x2 -> x0, waiting for transfers between devices: 258 us -> none  [the longest x1 151 us: body(): lax.all_to_all(grad_send, 'expert', split_axis=0, concat_axis=0, tiled=True)]
    all_to_all x1 -> x0, blocking collectives: 172 us -> none  [body(): lax.all_to_all(back, 'expert', split_axis=0, concat_axis=0, tiled=True)]
    scatter x2 -> x0, local copies, waits for them, and re-layouts: 59.3 us -> none  [the longest x1 35.3 us: body(): grad_send = empty.at[flat_ids, :, rank].set(scaled.reshape(-1, 2, half))]
    all_to_all x2 -> x0, starting transfers between devices: 30.3 us -> none  [the longest x1 19.8 us: body(): lax.all_to_all(tok_send, 'expert', split_axis=0, concat_axis=0, tiled=True)]
    reshape x7 -> x0, local copies, waits for them, and re-layouts: 24.5 us -> none  [the longest x1 4.49 us: body(): grad_flat = grad_in.reshape(sources * slots, half)]
    ppermute x3 -> x0, waiting for transfers between devices: 21.6 us -> none  [partner(): return lax.ppermute(value, axis, pairs)]
    dot_general x3 -> x0, matrix products: 15.9 us -> none  [the longest x1 5.87 us: body(): lax.dot_general(act_grad, w_in_full, (((1,), (1,)), ((), ())), preferred_...]
  transfers between devices with their start and end apart: 7 -> 0, of which waited for: 4 -> 0; matrix products, arithmetic and copies ran while one was open for 11% -> 0% of each run, Pallas kernels for 0% -> 0%
where the time goes in v1:
time: 293 us; the launch traced here: 292 us
  Pallas kernels  290 us (99%)
    pallas_call x1, Pallas kernels, call(): pl.pallas_call(functools.partial(kernel, ring, n_dp), out_shape=jax.Shape...  290 us

profile of v1, /device:TPU:1, one launch (start us, length us, event | category | flops | bytes accessed | tf_op | source)
XLA Modules:
  0.0 292.2 jit_solution(2324868854731629110)
XLA Ops:
  0.0 290.0 %routed_backward.1 = bf16[128,3584]{1,0:T(8,128)(2,1)} custom-call(bf16[128,3584]{1,0:T(8,128)(2,1)} %bitcast.12, bf16[128,3584]{1,0:T(8,128)(2,1)} %bitcast.13, s32[2,128]{1,0:T(2,128)} %bitcast.16, f32[2,128]{1,0:T(2,128)} %bitcast.17, bf16[1792,256]{1,0:T(8,128)(2,1)} %bitcast.14, bf16[1792,256]{1,0:T(8,128)(2,1)} %bitcast.15), custom_call_target="tpu_custom_call" | custom-call | tf_op jit(solution)/shard_map/routed_backward/pallas_call | solution.py:425
  290.0 2.2 copy.8

commit v2 on v1

--- a/solution.py
+++ b/solution.py
@@ -11,6 +11,7 @@
 F32 = jnp.float32
 BF16 = jnp.bfloat16
 GROUP = 8
+REACH = 2
 
 
 def silu_slope(pre):
@@ -56,57 +57,85 @@
     home_b_sem,
     hand_send_sem,
     hand_recv_sem,
-    wdp_send_sem,
-    wdp_recv_sem,
-    wcore_send_sem,
-    wcore_recv_sem,
+    wz_send_sem,
+    wz_recv_sem,
+    wy_send_sem,
+    wy_recv_sem,
 ):
     n_tok, width = tok_ref.shape
     half = width // 2
     quarter = win_ref.shape[1]
     chips = 2 * ring
+    far = ring // 2
     chunks = chips // GROUP
     section = lax.axis_index("section")
     me = lax.axis_index("expert")
     dp = lax.axis_index("dp")
-    core = lax.rem(me, 2)
-    my_chip = me // 2
-    my_xh = lax.rem(my_chip, 2)
-    my_z = my_chip // 2
+    core = me % 2
+    my_xh = me // 2 % 2
+    my_z = me // 4
     other_section = 1 - section
-    other_core = me + 1 - 2 * core
+    dp_up, dp_down = (dp + 1) % n_dp, (dp + n_dp - 1) % n_dp
+
+    side = 1 - 2 * core
+    host_z = (my_z + REACH * side + ring) % ring
+    host_chip = 2 * host_z + my_xh
+
+    def index_of(z, xh, which_core):
+        return 4 * ((z + 2 * ring) % ring) + 2 * xh + which_core
+
+    def steps_of(place):
+        odd = place % 2
+        hop = far - (place + odd) // 2
+        return jnp.where((odd == 1) | (place == 0), hop, -hop)
+
+    def target_of(unit):
+        d = steps_of(unit // 2)
+        to_side = jnp.where(
+            d == far, core, jnp.where(d == 0, 1 - core, (d < 0).astype(jnp.int32))
+        )
+        expert = index_of(my_z + d - REACH * (1 - 2 * to_side), unit % 2, to_side)
+        even = (d == far) | (d == 0)
+        spot = jnp.where(
+            even,
+            jnp.where(d == 0, 2, 0) + my_xh,
+            4 * (far - jnp.abs(d)) + 2 * core + my_xh,
+        )
+        return expert, spot
+
+    def source_of(spot):
+        step = spot // 4
+        d = jnp.where(step == 0, jnp.where(spot < 2, far, 0), side * (far - step))
+        their_core = jnp.where(
+            step == 0, jnp.where(spot < 2, core, 1 - core), spot // 2 % 2
+        )
+        return index_of(host_z - d, spot % 2, their_core)
 
     barrier = pltpu.get_barrier_semaphore()
 
+    def greet(**where):
+        pl.semaphore_signal(barrier, inc=1, device_id=where, device_id_type=MESH)
+
+    for where in (0, 1):
+        greet(expert=index_of(host_z, my_xh, where))
+    for where in (dp_up, dp_down):
+        greet(dp=where)
+    greet(section=other_section)
+
     @pl.loop(0, chips)
-    def _(chip):
-        @pl.when(chip != my_chip)
+    def _(i):
+        expert = source_of(i)
+
+        @pl.when(expert != me)
         def _():
-            pl.semaphore_signal(
-                barrier, inc=1, device_id={"expert": 2 * chip + core}, device_id_type=MESH
-            )
-
-        pl.semaphore_signal(
-            barrier,
-            inc=1,
-            device_id={"section": other_section, "expert": 2 * chip + core},
-            device_id_type=MESH,
-        )
-
-    for step in range(1, n_dp):
-        pl.semaphore_signal(
-            barrier, inc=1, device_id={"dp": lax.rem(dp + step, n_dp)}, device_id_type=MESH
-        )
-    pl.semaphore_signal(barrier, inc=1, device_id={"expert": other_core}, device_id_type=MESH)
+            greet(expert=expert)
+
+        greet(section=other_section, expert=target_of(i)[0])
 
     load_tok = pltpu.make_async_copy(tok_ref, xg.at[pl.ds(0, n_tok)], load_sem.at[0])
     load_grad = pltpu.make_async_copy(grad_ref, xg.at[pl.ds(n_tok, n_tok)], load_sem.at[1])
-    load_win = pltpu.make_async_copy(win_ref, w_full.at[dp, core], load_sem.at[2])
-    load_wout = pltpu.make_async_copy(wout_ref, v_full.at[dp, core], load_sem.at[3])
     load_tok.start()
     load_grad.start()
-    load_win.start()
-    load_wout.start()
 
     ids = jnp.concatenate([ids_ref[0:1, :], ids_ref[1:2, :]], axis=1)
     flat = 2 * n_tok
@@ -119,7 +148,7 @@
     rank = jnp.sum(hot * before, axis=0, keepdims=True).astype(jnp.int32)
     apart = (ids // 2 - my_z + ring) % ring
     hops = jnp.minimum(apart, ring - apart)
-    place = 2 * (ring // 2 - hops) - (apart < ring // 2).astype(jnp.int32)
+    place = 2 * (far - hops) - (apart < far).astype(jnp.int32)
     unit = 2 * place + ids % 2
     extra = rank >= GROUP
     full_rows = chips * 2 * GROUP
@@ -132,33 +161,34 @@
     picks = (slot_iota == slot[:, :n_tok]).astype(F32) + (slot_iota == slot[:, n_tok:]).astype(F32)
     combine[...] = jnp.transpose(picks).astype(BF16)
 
-    pl.semaphore_wait(barrier, 2 * chips - 1 + n_dp)
-
-    def weight_send(mat, y_from, target, to_core):
-        full = (w_full, v_full)[mat]
-        if to_core:
-            return pltpu.make_async_remote_copy(
-                src_ref=full.at[y_from, core],
-                dst_ref=full.at[y_from, core],
-                send_sem=wcore_send_sem.at[mat, y_from],
-                recv_sem=wcore_recv_sem.at[mat, y_from],
-                device_id={"expert": other_core},
-                device_id_type=MESH,
-            )
+    pl.semaphore_wait(barrier, 2 * chips - 1 + 5)
+
+    def weight_send(mat, to_side):
         return pltpu.make_async_remote_copy(
             src_ref=(win_ref, wout_ref)[mat],
-            dst_ref=full.at[dp, core],
-            send_sem=wdp_send_sem.at[mat, target],
-            recv_sem=wdp_recv_sem.at[mat, dp],
-            device_id={"dp": target},
+            dst_ref=(w_full, v_full)[mat].at[dp, core],
+            send_sem=wz_send_sem.at[mat, to_side],
+            recv_sem=wz_recv_sem.at[mat, core],
+            device_id={
+                "expert": index_of(my_z - REACH * (1 - 2 * to_side), my_xh, to_side)
+            },
             device_id_type=MESH,
         )
 
-    steps = [s for pair in zip(range(1, n_dp), range(n_dp - 1, 0, -1)) for s in pair]
-    steps = list(dict.fromkeys(steps))
-    for step in steps:
-        for mat in range(2):
-            weight_send(mat, None, lax.rem(dp + step, n_dp), False).start()
+    def weight_pass(mat, h, of_dp, up):
+        part = (w_full, v_full)[mat].at[of_dp, h]
+        return pltpu.make_async_remote_copy(
+            src_ref=part,
+            dst_ref=part,
+            send_sem=wy_send_sem.at[mat, h, of_dp, up],
+            recv_sem=wy_recv_sem.at[mat, h, of_dp],
+            device_id={"dp": dp_up if up else dp_down},
+            device_id_type=MESH,
+        )
+
+    for mat in range(2):
+        for to_side in range(2):
+            weight_send(mat, to_side).start()
 
     def hand(which):
         return pltpu.make_async_remote_copy(
@@ -176,44 +206,29 @@
     load_tok.wait()
     load_grad.wait()
 
-    def shift_of(place):
-        odd = place % 2
-        hop = ring // 2 - (place + odd) // 2
-        return jnp.where(odd == 1, hop, ring - hop) % ring
-
-    def mirror_of(place):
-        odd = place % 2
-        inner = jnp.where(odd == 1, place + 1, place - 1)
-        return jnp.where((place == 0) | (place == ring - 1), place, inner)
-
     def dispatch(unit, own):
-        place = unit // 2
-        xh = unit % 2
-        chip = 2 * ((my_z + shift_of(place)) % ring) + xh
-        there = 2 * mirror_of(place) + my_xh
-        pair_a = (send_a.at[unit], recv_a.at[there // GROUP, there % GROUP])
-        pair_b = (send_b.at[unit], recv_b.at[there])
+        expert, spot = target_of(unit)
         pairs = (
-            (pair_a, (send_a_sem, recv_a_sem)),
-            (pair_b, (send_b_sem, recv_b_sem)),
+            (send_a.at[unit], recv_a.at[spot // GROUP, spot % GROUP], send_a_sem, recv_a_sem),
+            (send_b.at[unit], recv_b.at[spot], send_b_sem, recv_b_sem),
         )
         if own:
             return [
-                pltpu.make_async_copy(*pair, sems[1].at[there]) for pair, sems in pairs
+                pltpu.make_async_copy(source, place, arrived.at[spot])
+                for source, place, _, arrived in pairs
             ]
         return [
             pltpu.make_async_remote_copy(
-                src_ref=pair[0],
-                dst_ref=pair[1],
-                send_sem=sems[0].at[unit],
-                recv_sem=sems[1].at[there],
-                device_id={"expert": 2 * chip + core},
+                src_ref=source,
+                dst_ref=place,
+                send_sem=sent.at[unit],
+                recv_sem=arrived.at[spot],
+                device_id={"expert": expert},
                 device_id_type=MESH,
             )
-            for pair, sems in pairs
+            for source, place, sent, arrived in pairs
         ]
 
-    own_unit = 2 * (ring - 1) + my_xh
     rows = GROUP * 2 * GROUP
     block = 512 if width % 512 == 0 else 256
 
@@ -247,7 +262,7 @@
         @pl.loop(0, GROUP)
         def _(i):
             unit = chunk * GROUP + i
-            own = unit == own_unit
+            own = target_of(unit)[0] == me
 
             @pl.when(own)
             def _():
@@ -259,48 +274,40 @@
                 for copy in dispatch(unit, False):
                     copy.start()
 
-    load_win.wait()
-    load_wout.wait()
+    def weight_arrive(mat, h, of_dp, sem):
+        part = (w_full, v_full)[mat].at[of_dp, h]
+        pltpu.make_async_copy(part, part, sem).wait()
+
     for mat in range(2):
-        weight_send(mat, dp, None, True).start()
-    for step in steps:
-        y_from = lax.rem(dp + n_dp - step, n_dp)
+        for h in range(2):
+            weight_arrive(mat, h, dp, wz_recv_sem.at[mat, h])
+            for up in range(2):
+                weight_pass(mat, h, dp, up).start()
+    for h in range(2):
+        weight_arrive(0, h, dp_down, wy_recv_sem.at[0, h, dp_down])
+        weight_pass(0, h, dp_down, 1).start()
+        weight_arrive(1, h, dp_up, wy_recv_sem.at[1, h, dp_up])
+        weight_pass(1, h, dp_up, 0).start()
+    for h in range(2):
+        weight_arrive(0, h, dp_up, wy_recv_sem.at[0, h, dp_up])
+        weight_arrive(1, h, dp_down, wy_recv_sem.at[1, h, dp_down])
         for mat in range(2):
-            pltpu.make_async_remote_copy(
-                src_ref=(win_ref, wout_ref)[mat],
-                dst_ref=(w_full, v_full)[mat].at[y_from, core],
-                send_sem=wdp_send_sem.at[mat, y_from],
-                recv_sem=wdp_recv_sem.at[mat, y_from],
-                device_id={"dp": y_from},
-                device_id_type=MESH,
-            ).wait_recv()
-            weight_send(mat, y_from, None, True).start()
-    for y_from in range(n_dp):
-        for mat in range(2):
-            full = (w_full, v_full)[mat]
-            pltpu.make_async_remote_copy(
-                src_ref=full.at[y_from, 1 - core],
-                dst_ref=full.at[y_from, 1 - core],
-                send_sem=wcore_send_sem.at[mat, y_from],
-                recv_sem=wcore_recv_sem.at[mat, y_from],
-                device_id={"expert": other_core},
-                device_id_type=MESH,
-            ).wait_recv()
+            opposite = (dp + 2) % n_dp
+            weight_arrive(mat, h, opposite, wy_recv_sem.at[mat, h, opposite])
 
     def give_back(unit):
-        chip = 2 * ((my_z + shift_of(unit // 2)) % ring) + unit % 2
         return [
             pltpu.make_async_remote_copy(
                 src_ref=source.at[unit],
-                dst_ref=home.at[my_chip],
-                send_sem=sems[0].at[unit],
-                recv_sem=sems[1].at[my_chip],
-                device_id={"section": other_section, "expert": 2 * chip + core},
+                dst_ref=home.at[host_chip],
+                send_sem=sent.at[unit],
+                recv_sem=arrived.at[host_chip],
+                device_id={"section": other_section, "expert": source_of(unit)},
                 device_id_type=MESH,
             )
-            for source, home, sems in (
-                (back_a, home_a, (back_a_sem, home_a_sem)),
-                (back_b, home_b, (back_b_sem, home_b_sem)),
+            for source, home, sent, arrived in (
+                (back_a, home_a, back_a_sem, home_a_sem),
+                (back_b, home_b, back_b_sem, home_b_sem),
             )
         ]
 
@@ -325,13 +332,13 @@
 
         @pl.loop(0, n_dp)
         def _(y):
-            def product(full, first):
+            def product(full, offset):
                 total = None
                 for h in range(2):
                     left = recv_a[chunk, :, :, h * half : (h + 1) * half].reshape(tall, half)
                     part = jnp.dot(left, full[y, h], preferred_element_type=F32)
                     part = part.reshape(GROUP + 1, 2 * GROUP, quarter)
-                    part = part[:, first : first + GROUP, :].astype(BF16).astype(F32)
+                    part = part[:, offset : offset + GROUP, :].astype(BF16).astype(F32)
                     total = part if total is None else total + part
                 return total
 
@@ -394,16 +401,19 @@
 
     hand(0).wait_send()
     hand(1).wait_send()
-    for step in range(1, n_dp):
-        for mat in range(2):
-            weight_send(mat, None, lax.rem(dp + step, n_dp), False).wait_send()
-    for y_from in range(n_dp):
-        for mat in range(2):
-            weight_send(mat, y_from, None, True).wait_send()
+    for mat in range(2):
+        for to_side in range(2):
+            weight_send(mat, to_side).wait_send()
+        for h in range(2):
+            for up in range(2):
+                weight_pass(mat, h, dp, up).wait_send()
+    for h in range(2):
+        weight_pass(0, h, dp_down, 1).wait_send()
+        weight_pass(1, h, dp_up, 0).wait_send()
 
     @pl.loop(0, chips)
     def _(unit):
-        @pl.when(unit != own_unit)
+        @pl.when(target_of(unit)[0] != me)
         def _():
             for copy in dispatch(unit, False):
                 copy.wait_send()
@@ -445,7 +455,7 @@
             pltpu.VMEM((n_dp, GROUP * (GROUP + 1), quarter), BF16),
             pltpu.VMEM((2 * GROUP, width), F32),
             pltpu.VMEM((chips, width), F32),
-            dma((4,)),
+            dma((2,)),
             dma((chips,)),
             dma((chips,)),
             dma((chips,)),
@@ -456,10 +466,10 @@
             dma((chips,)),
             dma((2,)),
             dma((2,)),
-            dma((2, n_dp)),
-            dma((2, n_dp)),
-            dma((2, n_dp)),
-            dma((2, n_dp)),
+            dma((2, 2)),
+            dma((2, 2)),
+            dma((2, 2, n_dp, 2)),
+            dma((2, 2, n_dp)),
         ],
         compiler_params=pltpu.CompilerParams(
             collective_id=0, has_side_effects=True, vmem_limit_bytes=56 * 1024 * 1024

time: 293 us -> 280 us (0.956)
  Pallas kernels: 290 us -> 278 us
    pallas_call x1, Pallas kernels: 290 us -> 278 us  [call(): pl.pallas_call(functools.partial(kernel, ring, n_dp), out_shape=jax.Shape...]
where the time goes in v2:
time: 280 us
  Pallas kernels  278 us (99%)
    pallas_call x1, Pallas kernels, call(): pl.pallas_call(functools.partial(kernel, ring, n_dp), out_shape=jax.Shape...  278 us

profile of v2, /device:TPU:1, one launch (start us, length us, event | category | flops | bytes accessed | tf_op | source)
XLA Modules:
  0.0 279.9 jit_solution(11749416456437418341)
XLA Ops:
  0.0 277.7 %routed_backward.1 = bf16[128,3584]{1,0:T(8,128)(2,1)} custom-call(bf16[128,3584]{1,0:T(8,128)(2,1)} %bitcast.12, bf16[128,3584]{1,0:T(8,128)(2,1)} %bitcast.13, s32[2,128]{1,0:T(2,128)} %bitcast.16, f32[2,128]{1,0:T(2,128)} %bitcast.17, bf16[1792,256]{1,0:T(8,128)(2,1)} %bitcast.14, bf16[1792,256]{1,0:T(8,128)(2,1)} %bitcast.15), custom_call_target="tpu_custom_call" | custom-call | tf_op jit(solution)/shard_map/routed_backward/pallas_call | solution.py:435
  277.7 2.2 copy.8

commit v3 on v2

--- a/solution.py
+++ b/solution.py
@@ -85,6 +85,7 @@
         return 4 * ((z + 2 * ring) % ring) + 2 * xh + which_core
 
     def steps_of(place):
+        place = (place + ring - 1) % ring
         odd = place % 2
         hop = far - (place + odd) // 2
         return jnp.where((odd == 1) | (place == 0), hop, -hop)
@@ -148,7 +149,7 @@
     rank = jnp.sum(hot * before, axis=0, keepdims=True).astype(jnp.int32)
     apart = (ids // 2 - my_z + ring) % ring
     hops = jnp.minimum(apart, ring - apart)
-    place = 2 * (far - hops) - (apart < far).astype(jnp.int32)
+    place = (2 * (far - hops) - (apart < far).astype(jnp.int32) + 1) % ring
     unit = 2 * place + ids % 2
     extra = rank >= GROUP
     full_rows = chips * 2 * GROUP
@@ -232,8 +233,17 @@
     rows = GROUP * 2 * GROUP
     block = 512 if width % 512 == 0 else 256
 
-    @pl.loop(0, chunks)
-    def _(chunk):
+    def weight_arrive(mat, h, of_dp, sem):
+        part = (w_full, v_full)[mat].at[of_dp, h]
+        pltpu.make_async_copy(part, part, sem).wait()
+
+    for mat in range(2):
+        for h in range(2):
+            weight_arrive(mat, h, dp, wz_recv_sem.at[mat, h])
+            for up in range(2):
+                weight_pass(mat, h, dp, up).start()
+
+    def send_rows(chunk):
         local_row = lax.broadcasted_iota(jnp.int32, (rows + 2 * GROUP, 1), 0)
         spare = local_row >= rows
         row_id = jnp.where(
@@ -274,20 +284,17 @@
                 for copy in dispatch(unit, False):
                     copy.start()
 
-    def weight_arrive(mat, h, of_dp, sem):
-        part = (w_full, v_full)[mat].at[of_dp, h]
-        pltpu.make_async_copy(part, part, sem).wait()
-
-    for mat in range(2):
-        for h in range(2):
-            weight_arrive(mat, h, dp, wz_recv_sem.at[mat, h])
-            for up in range(2):
-                weight_pass(mat, h, dp, up).start()
+    send_rows(0)
     for h in range(2):
         weight_arrive(0, h, dp_down, wy_recv_sem.at[0, h, dp_down])
         weight_pass(0, h, dp_down, 1).start()
         weight_arrive(1, h, dp_up, wy_recv_sem.at[1, h, dp_up])
         weight_pass(1, h, dp_up, 0).start()
+
+    @pl.loop(1, chunks)
+    def _(chunk):
+        send_rows(chunk)
+
     for h in range(2):
         weight_arrive(0, h, dp_up, wy_recv_sem.at[0, h, dp_up])
         weight_arrive(1, h, dp_down, wy_recv_sem.at[1, h, dp_down])

time: 280 us -> 273 us (0.975)
  Pallas kernels: 278 us -> 270 us
    pallas_call x1, Pallas kernels: 278 us -> 270 us  [call(): pl.pallas_call(functools.partial(kernel, ring, n_dp), out_shape=jax.Shape...]
where the time goes in v3:
time: 273 us; the launch traced here: 272 us
  Pallas kernels  270 us (99%)
    pallas_call x1, Pallas kernels, call(): pl.pallas_call(functools.partial(kernel, ring, n_dp), out_shape=jax.Shape...  270 us

profile of v3, /device:TPU:1, one launch (start us, length us, event | category | flops | bytes accessed | tf_op | source)
XLA Modules:
  0.0 272.3 jit_solution(1955946872561548503)
XLA Ops:
  0.0 270.2 %routed_backward.1 = bf16[128,3584]{1,0:T(8,128)(2,1)} custom-call(bf16[128,3584]{1,0:T(8,128)(2,1)} %bitcast.12, bf16[128,3584]{1,0:T(8,128)(2,1)} %bitcast.13, s32[2,128]{1,0:T(2,128)} %bitcast.16, f32[2,128]{1,0:T(2,128)} %bitcast.17, bf16[1792,256]{1,0:T(8,128)(2,1)} %bitcast.14, bf16[1792,256]{1,0:T(8,128)(2,1)} %bitcast.15), custom_call_target="tpu_custom_call" | custom-call | tf_op jit(solution)/shard_map/routed_backward/pallas_call | solution.py:442
  270.2 2.2 copy.8

commit v4 on v3

--- a/solution.py
+++ b/solution.py
@@ -290,8 +290,16 @@
         weight_pass(0, h, dp_down, 1).start()
         weight_arrive(1, h, dp_up, wy_recv_sem.at[1, h, dp_up])
         weight_pass(1, h, dp_up, 0).start()
-
-    @pl.loop(1, chunks)
+    send_rows(1)
+
+    @pl.loop(0, GROUP)
+    def _(unit):
+        @pl.when(target_of(unit)[0] != me)
+        def _():
+            for copy in dispatch(unit, False):
+                copy.wait_send()
+
+    @pl.loop(2, chunks)
     def _(chunk):
         send_rows(chunk)
 
@@ -389,11 +397,10 @@
         pltpu.make_async_copy(a_ref, a_ref, home_a_sem.at[chip]).wait()
         b_ref = home_b.at[chip]
         pltpu.make_async_copy(b_ref, b_ref, home_b_sem.at[chip]).wait()
-
-    for chip in range(chips):
         pair = home_b[chip].astype(F32)
-        home_scr[chip : chip + 1, :half] = pair[0:1]
-        home_scr[chip : chip + 1, half:] = pair[1:2]
+        home_scr[pl.ds(chip, 1), :half] = pair[0:1]
+        home_scr[pl.ds(chip, 1), half:] = pair[1:2]
+
     for lane in range(0, width, block):
         span = slice(lane, lane + block)
         main = home_a[:, :, span].astype(F32).reshape(chips * GROUP, block).astype(BF16)
@@ -420,7 +427,7 @@
 
     @pl.loop(0, chips)
     def _(unit):
-        @pl.when(target_of(unit)[0] != me)
+        @pl.when((unit >= GROUP) & (target_of(unit)[0] != me))
         def _():
             for copy in dispatch(unit, False):
                 copy.wait_send()

time: 273 us -> 273 us (level)
  no operation moved by 1% of the time
where the time goes in v4:
time: 273 us; the launch traced here: 272 us
  Pallas kernels  270 us (99%)
    pallas_call x1, Pallas kernels, call(): pl.pallas_call(functools.partial(kernel, ring, n_dp), out_shape=jax.Shape...  270 us

profile of v4, /device:TPU:1, one launch (start us, length us, event | category | flops | bytes accessed | tf_op | source)
XLA Modules:
  0.0 272.4 jit_solution(7263362672562697590)
XLA Ops:
  0.0 270.2 %routed_backward.1 = bf16[128,3584]{1,0:T(8,128)(2,1)} custom-call(bf16[128,3584]{1,0:T(8,128)(2,1)} %bitcast.12, bf16[128,3584]{1,0:T(8,128)(2,1)} %bitcast.13, s32[2,128]{1,0:T(2,128)} %bitcast.16, f32[2,128]{1,0:T(2,128)} %bitcast.17, bf16[1792,256]{1,0:T(8,128)(2,1)} %bitcast.14, bf16[1792,256]{1,0:T(8,128)(2,1)} %bitcast.15), custom_call_target="tpu_custom_call" | custom-call | tf_op jit(solution)/shard_map/routed_backward/pallas_call | solution.py:449
  270.2 2.2 copy.8
